TPU v7x, 256 devices: a whole 4x4x8 slice. The times are simulated.
256 devices in a mesh: nodes: 128 (over y, z, x), rep: 2 (over core).
Axes of the slice: x: 4, y: 4, z: 8, core: 2. Of those that a mesh axis runs over, the one named last changes fastest.
Arguments:
- node_latent: bfloat16 [40960, 512], P(('nodes', 'rep')), may hold values from -6 to 6
- edge_saved: bfloat16 [327680, 512], P(('nodes', 'rep')), may hold values from -6 to 6
- node_cot: bfloat16 [40960, 512], P(('nodes', 'rep')), may hold values from -6 to 6
- edge_cot: bfloat16 [327680, 512], P(('nodes', 'rep')), may hold values from -6 to 6
- senders: int32 [327680], P(('nodes', 'rep')), may hold values from 0 to 1343, as said below
- receivers: int32 [327680], P(('nodes', 'rep')), may hold values from 0 to 319
- ghost_rows: int32 [128, 128, 8], P('nodes'), may hold values from 0 to 319, as said below
- w_edge_in: bfloat16 [1536, 512], replicated, may hold values from -0.15625 to 0.15625
- w_edge_out: bfloat16 [512, 512], replicated, may hold values from -0.25 to 0.25
- edge_gain: float32 [512], replicated, may hold values from 0.5 to 2
- edge_offset: float32 [512], replicated, may hold values from -3 to 3
- w_node_in: bfloat16 [1024, 512], replicated, may hold values from -0.1875 to 0.1875
- w_node_out: bfloat16 [512, 512], replicated, may hold values from -0.25 to 0.25
- node_gain: float32 [512], replicated, may hold values from 0.5 to 2
Outputs:
- grad_nodes: bfloat16 [40960, 512], P(('nodes', 'rep'))
- grad_edges: bfloat16 [327680, 512], P(('nodes', 'rep'))
- grad_edge_in: bfloat16 [1536, 512], replicated
- grad_edge_out: bfloat16 [512, 512], replicated
- grad_node_in: bfloat16 [1024, 512], replicated
- grad_node_out: bfloat16 [512, 512], replicated
Inputs may be any that keep to these rules, and one draw needn't show every extreme that they name: `senders`: A sender below 320 is a node of the edge's own partition; otherwise it is 320 + q * 8 + s, the ghost slot s of the list of a partition q other than the edge's own. Each list ghost_rows[q, p] holds 8 distinct rows.
All inputs are finite; a program needn't handle non-finite values.
Results may differ from a plain program's by a relative error of at most 0.008.
Values may be sent and summed in bfloat16 or wider, within the bound.
No kernel may reach another device: no remote copies, remote signals or barrier semaphores. Data moves between devices by JAX's collectives and lax.ppermute only.
A program may use at most 128 MiB of HBM per device.

v0:
```python
import math
import jax
import jax.numpy as jnp
from jax import lax
from jax.sharding import PartitionSpec as P

EPS = 1e-05


def swapped(array, axis, bit):
    return lax.ppermute(array, axis, [(i, i ^ 1 << bit) for i in range(lax.axis_size(axis))])


def sent_to_all(array, axis):
    devices = lax.axis_size(axis)
    return lax.all_to_all(
        jnp.broadcast_to(array[None], (devices, *array.shape)), axis, 0, 0, tiled=True
    )


def in_order(blocks, dim):
    blocks = jnp.moveaxis(blocks, 0, dim)
    dims = blocks.shape
    return blocks.reshape(*dims[:dim], dims[dim] * dims[dim + 1], *dims[dim + 2 :])


def gather_directly(array, axis, dim):
    blocks = sent_to_all(array, axis)
    return in_order(blocks, dim)


def split_up(array, dim, devices):
    before, after = (array.shape[:dim], array.shape[dim + 1 :])
    return jnp.moveaxis(array.reshape(*before, devices, -1, *after), dim, 0)


def summed_on_arrival(array, axis, dim):
    devices = lax.axis_size(axis)
    blocks = lax.all_to_all(split_up(array, dim, devices), axis, 0, 0, tiled=True)
    return jnp.sum(blocks, axis=0)


def summed_on_arrival_2(array, axis, dim):
    devices = lax.axis_size(axis)
    blocks = lax.all_to_all(split_up(array, dim, devices), axis, 0, 0, tiled=True)
    return jnp.sum(blocks.astype(jnp.float32), axis=0)


def mat_mul(left, right):
    return jnp.dot(left, right, preferred_element_type=jnp.float32)


def mat_tn(left, right):
    return lax.dot_general(
        left, right, (((0,), (0,)), ((), ())), preferred_element_type=jnp.float32
    )


def mat_nt(left, right):
    return lax.dot_general(
        left, right, (((1,), (1,)), ((), ())), preferred_element_type=jnp.float32
    )


def silu_slope(value):
    sigmoid_v = jax.nn.sigmoid(value)
    return sigmoid_v * (1.0 + value * (1.0 - sigmoid_v))


def norm_forward(value):
    centred = value - jnp.mean(value, axis=-1, keepdims=True)
    inverse = lax.rsqrt(jnp.mean(centred * centred, axis=-1, keepdims=True) + EPS)
    return (centred * inverse, inverse)


def norm_backward(grad_hat, normed, inverse):
    return inverse * (
        grad_hat
        - jnp.mean(grad_hat, axis=-1, keepdims=True)
        - normed * jnp.mean(grad_hat * normed, axis=-1, keepdims=True)
    )


def edge_forward(edge_block, send_rows, recv_rows, w_edge_in, w_edge_out, edge_gain, edge_offset):
    latent_width = edge_block.shape[1]
    pre_act = (
        mat_mul(edge_block, w_edge_in[:latent_width])
        + mat_mul(send_rows, w_edge_in[latent_width : 2 * latent_width])
        + mat_mul(recv_rows, w_edge_in[2 * latent_width :])
    )
    edge_hidden = jax.nn.silu(pre_act).astype(jnp.bfloat16)
    edge_normed, edge_inverse = norm_forward(mat_mul(edge_hidden, w_edge_out))
    message = edge_normed * edge_gain + edge_offset
    return (pre_act, edge_hidden, edge_normed, edge_inverse, message)


def edge_backward(
    edge_block,
    send_rows,
    recv_rows,
    edge_cot,
    message_grad,
    saved,
    w_edge_in,
    w_edge_out,
    edge_gain,
):
    pre_act, edge_hidden, edge_normed, edge_inverse = saved
    latent_width = edge_block.shape[1]
    grad_out = norm_backward(message_grad * edge_gain, edge_normed, edge_inverse).astype(
        jnp.bfloat16
    )
    grad_act = (mat_nt(grad_out, w_edge_out) * silu_slope(pre_act)).astype(jnp.bfloat16)
    in_grad = jnp.concatenate(
        [mat_tn(edge_block, grad_act), mat_tn(send_rows, grad_act), mat_tn(recv_rows, grad_act)], 0
    )
    out_grad = mat_tn(edge_hidden, grad_out)
    edge_grad = (edge_cot.astype(jnp.float32) + mat_nt(grad_act, w_edge_in[:latent_width])).astype(
        jnp.bfloat16
    )
    send_grad = mat_nt(grad_act, w_edge_in[latent_width : 2 * latent_width])
    recv_grad = mat_nt(grad_act, w_edge_in[2 * latent_width :])
    return (edge_grad, send_grad, recv_grad, in_grad, out_grad)


def node_pass(node_rows, totals_b, node_cot, w_node_in, w_node_out, node_gain):
    latent_width = node_rows.shape[1]
    node_pre = mat_mul(node_rows, w_node_in[:latent_width]) + mat_mul(
        totals_b, w_node_in[latent_width:]
    )
    node_hidden = jax.nn.silu(node_pre).astype(jnp.bfloat16)
    node_normed, node_inverse = norm_forward(mat_mul(node_hidden, w_node_out))
    grad_out = norm_backward(
        node_cot.astype(jnp.float32) * node_gain, node_normed, node_inverse
    ).astype(jnp.bfloat16)
    grad_act = (mat_nt(grad_out, w_node_out) * silu_slope(node_pre)).astype(jnp.bfloat16)
    in_grad = jnp.concatenate([mat_tn(node_rows, grad_act), mat_tn(totals_b, grad_act)], 0)
    direct_grad = mat_nt(grad_act, w_node_in[:latent_width])
    totals_grad = mat_nt(grad_act, w_node_in[latent_width:]).astype(jnp.bfloat16)
    return (direct_grad, totals_grad, in_grad, mat_tn(node_hidden, grad_out))


def shards(
    node_latent,
    edge_saved,
    node_cot,
    edge_cot,
    senders,
    receivers,
    ghost_rows,
    w_edge_in,
    w_edge_out,
    edge_gain,
    edge_offset,
    w_node_in,
    w_node_out,
    node_gain,
):
    latent_width = node_latent.shape[1]
    edge_latent = swapped(edge_saved, "rep", 0)
    partition = gather_directly(node_latent, "rep", 0)
    part_rows = partition.shape[0]
    ghost_lists = ghost_rows[0]
    part_count = ghost_lists.shape[0]
    slot_count = ghost_lists.shape[1]
    half_slots = slot_count // lax.axis_size("rep")
    own_lists = lax.dynamic_slice_in_dim(
        ghost_lists, lax.axis_index("rep") * half_slots, half_slots, 1
    )
    outgoing = partition[own_lists.reshape(-1)].reshape(part_count, half_slots, latent_width)
    arrived = lax.all_to_all(outgoing, "nodes", split_axis=0, concat_axis=0, tiled=True)
    ghosts = gather_directly(arrived, "rep", 1)
    node_table = jnp.concatenate(
        [partition, ghosts.reshape(part_count * slot_count, latent_width)], 0
    )
    send_rows = node_table[senders]
    recv_rows = partition[receivers]
    pre_act, edge_hidden, edge_normed, edge_inverse, message = edge_forward(
        edge_latent, send_rows, recv_rows, w_edge_in, w_edge_out, edge_gain, edge_offset
    )
    partial_totals = jax.ops.segment_sum(message, receivers, num_segments=part_rows)
    totals = summed_on_arrival(partial_totals, "rep", 0)
    direct_grad, totals_grad, node_in_grad, node_out_grad = node_pass(
        node_latent, totals.astype(jnp.bfloat16), node_cot, w_node_in, w_node_out, node_gain
    )
    partition_totals_grad = gather_directly(totals_grad, "rep", 0)
    message_grad = edge_cot.astype(jnp.float32) + partition_totals_grad[receivers].astype(
        jnp.float32
    )
    edge_grad, send_grad, recv_grad, edge_in_grad, edge_out_grad = edge_backward(
        edge_latent,
        send_rows,
        recv_rows,
        edge_cot,
        message_grad,
        (pre_act, edge_hidden, edge_normed, edge_inverse),
        w_edge_in,
        w_edge_out,
        edge_gain,
    )
    table_grad = jax.ops.segment_sum(send_grad, senders, num_segments=node_table.shape[0])
    row_grad = table_grad[:part_rows] + jax.ops.segment_sum(
        recv_grad, receivers, num_segments=part_rows
    )
    ghost_grad = table_grad[part_rows:].reshape(part_count, slot_count, latent_width)
    paired = summed_on_arrival_2(ghost_grad.astype(jnp.bfloat16), "rep", 1)
    returned = lax.all_to_all(
        paired.astype(jnp.bfloat16), "nodes", split_axis=0, concat_axis=0, tiled=True
    ).astype(paired.dtype)
    row_grad = row_grad + jax.ops.segment_sum(
        returned.reshape(-1, latent_width), own_lists.reshape(-1), num_segments=part_rows
    )
    own_grad = summed_on_arrival(row_grad, "rep", 0)
    grad_nodes = (own_grad + direct_grad + node_cot.astype(jnp.float32)).astype(jnp.bfloat16)
    weight_grads = (edge_in_grad, edge_out_grad, node_in_grad, node_out_grad)
    device_count = lax.axis_size("nodes") * lax.axis_size("rep")
    edge_scale = 1.0 / math.sqrt(senders.shape[0] * device_count)
    node_scale = 1.0 / math.sqrt(node_latent.shape[0] * device_count)
    weight_total = lax.psum(
        (weight_grads[0], weight_grads[1], weight_grads[2], weight_grads[3]), ("nodes", "rep")
    )
    return (
        grad_nodes,
        edge_grad,
        (weight_total[0] * edge_scale).astype(jnp.bfloat16),
        (weight_total[1] * edge_scale).astype(jnp.bfloat16),
        (weight_total[2] * node_scale).astype(jnp.bfloat16),
        (weight_total[3] * node_scale).astype(jnp.bfloat16),
    )


def solution(mesh):
    return jax.shard_map(
        shards,
        mesh=mesh,
        in_specs=(
            P(("nodes", "rep"), None),
            P(("nodes", "rep"), None),
            P(("nodes", "rep"), None),
            P(("nodes", "rep"), None),
            P(("nodes", "rep")),
            P(("nodes", "rep")),
            P("nodes", None, None),
            P(),
            P(),
            P(),
            P(),
            P(),
            P(),
            P(),
        ),
        out_specs=(P(("nodes", "rep"), None), P(("nodes", "rep"), None), P(), P(), P(), P()),
        check_vma=False,
    )
```

profile of v0, /device:TPU:2, one launch (start us, length us, event | category | flops | bytes accessed | tf_op | source)
XLA Modules:
  0.0 423.5 jit_solution(2287839622179952610)
XLA Ops:
  7.2 1.7 broadcast_in_dim.18
  8.9 3.5 all-to-all-start
  12.4 0.7 constant_dynamic-slice_fusion
  13.3 0.6 all-to-all-done
  14.0 2.0 gather_fusion
  15.9 0.9 reshape.119
  16.8 15.9 %all-to-all-start.1 = ((bf16[128,4,512]{2,1,0:T(4,128)(2,1)}), bf16[128,4,512]{2,1,0:T(4,128)(2,1)}, u32[]{:S(2)}, u32[]{:S(2)}) async-start(bf16[128,4,512]{2,1,0:T(4,128)(2,1)} %reshape.119), calls=%async_computation.1 | async-start | bytes 1048576 | tf_op jit(solution)/shard_map/all_to_all | solution.py:171
  32.9 4.1 gather_fusion.2
  37.1 2.9 copy.33
  40.0 0.6 pad_clamp_fusion.1
  40.6 1.0 fusion.13
  41.6 3.4 fusion.17
  45.0 6.5 %all-to-all-done.1 = bf16[128,4,512]{2,1,0:T(4,128)(2,1)} async-done(((bf16[128,4,512]{2,1,0:T(4,128)(2,1)}), bf16[128,4,512]{2,1,0:T(4,128)(2,1)}, u32[]{:S(2)}, u32[]{:S(2)}) %all-to-all-start.1) | async-done | bytes 524320 | tf_op jit(solution)/shard_map/all_to_all | solution.py:171
  51.5 1.3 broadcast_in_dim.19
  52.8 5.1 %all_to_all.40 = bf16[2,128,4,512]{3,2,1,0:T(4,128)(2,1)S(1)} all-to-all(bf16[2,128,4,512]{3,2,1,0:T(4,128)(2,1)S(1)} %broadcast_in_dim.19), channel_id=1, replica_groups=mesh['nodes'=128,'rep'=2] {'rep'}, dimensions={0} | all-to-all | bytes 2097152 | tf_op jit(solution)/shard_map/all_to_all | solution.py:16
  58.7 4.2 %gather_fusion.1 = bf16[1280,512]{1,0:T(8,128)(2,1)S(1)} fusion(bf16[1344,512]{1,0:T(8,128)(2,1)S(1)} %pad_maximum_fusion.2, s32[2048]{0:T(1024)} %pad_clamp_fusion.1), kind=kCustom, calls=%fused_computation.1 | custom fusion | bytes 2626560 | tf_op jit(solution)/shard_map/gather | solution.py:176
  62.9 2.4 fusion.21
  65.4 4.2 %multiply_convert_fusion.2 = (bf16[1280,512]{1,0:T(8,128)(2,1)S(1)}, f32[1280,512]{1,0:T(8,128)}) fusion(f32[1280,512]{1,0:T(8,128)S(1)} %copy-done.10, f32[1280,512]{1,0:T(8,128)S(1)} %fusion.21, bf16[1280,512]{1,0:T(8,128)(2,1)} %collective-permute-done, bf16[1536,512]{1,0:T(8,128)(2,1)} %param.21), kind=kOutput, calls=%fused_computation.22 | convolution fusion | flops 675676160 | bytes 11010048 | tf_op jit(solution)/shard_map/dot_general | solution.py:50
  69.6 0.9 fusion.43
  70.9 1.9 multiply_add_fusion
  72.8 3.2 copy.34
  76.0 11.1 %scatter_custom_fusion = f32[320,512]{1,0:T(8,128)} fusion(s32[1280]{0:T(1024)S(1)} %copy-done.35, f32[1280,512]{1,0:T(8,128)} %copy.34, f32[]{:T(128)} %constant.13.clone.1), kind=kCustom, calls=%fused_computation.72 | custom fusion | flops 655360 | bytes 655872 | tf_op jit(solution)/shard_map/scatter-add | solution.py:181
  87.1 6.4 %all_to_all.41 = f32[2,160,512]{2,1,0:T(8,128)} all-to-all(f32[2,160,512]{2,1,0:T(8,128)} %bitcast.47), channel_id=1, replica_groups=mesh['nodes'=128,'rep'=2] {'rep'}, dimensions={0} | all-to-all | bytes 1310720 | tf_op jit(solution)/shard_map/all_to_all | solution.py:39
  93.5 1.2 reduce_sum.104
  94.7 1.5 convolution_add_fusion.3
  96.2 1.5 fusion.44
  99.3 4.2 all_to_all.42
  103.5 4.7 %gather_fusion.3 = bf16[1280,512]{1,0:T(8,128)(2,1)} fusion(bf16[320,512]{1,0:T(8,128)(2,1)S(1)} %bitcast.44, s32[2048]{0:T(1024)S(1)} %pad_clamp_fusion), kind=kCustom, calls=%fused_computation.3 | custom fusion | bytes 2626560 | tf_op jit(solution)/shard_map/gather | solution.py:187
  108.2 2.4 copy.35
  110.6 2.7 fusion.4
  113.3 1.0 multiply_convert_fusion.1
  114.3 0.7 copy-done.45
  115.1 1.5 fusion.2
  116.6 0.9 fusion.46
  117.5 0.9 copy-done.8
  118.4 0.9 fusion.45
  119.3 0.5 copy-done.24
  119.7 1.9 fusion.47
  122.8 1.4 fusion.39
  124.2 1.5 pad_maximum_fusion.1
  125.7 2.2 convolution_bitcast_fusion
  127.9 2.0 pad_maximum_fusion
  129.9 3.5 fusion.19
  133.4 11.1 %scatter_custom_fusion.1 = f32[1344,512]{1,0:T(8,128)S(1)} fusion(s32[1280]{0:T(1024)} %param.18, f32[1280,512]{1,0:T(8,128)} %fusion.19, f32[]{:T(128)} %constant.13.clone.1), kind=kCustom, calls=%fused_computation.30 | custom fusion | flops 655360 | bytes 2753024 | tf_op jit(solution)/shard_map/scatter-add | solution.py:201
  144.5 1.3 slice.65
  145.8 2.2 convert_element_type.72
  147.9 1.6 copy.42
  149.6 5.6 %all_to_all.43 = bf16[2,128,4,512]{3,2,1,0:T(4,128)(2,1)} all-to-all(bf16[2,128,4,512]{3,2,1,0:T(4,128)(2,1)S(1)} %bitcast.46), channel_id=1, replica_groups=mesh['nodes'=128,'rep'=2] {'rep'}, dimensions={0} | all-to-all | bytes 2097152 | tf_op jit(solution)/shard_map/all_to_all | solution.py:45
  155.2 2.9 reduce_sum.111
  158.1 8.1 %all-to-all-start.6 = ((bf16[128,4,512]{2,1,0:T(4,128)(2,1)}), bf16[128,4,512]{2,1,0:T(4,128)(2,1)}, u32[]{:S(2)}, u32[]{:S(2)}) async-start(bf16[128,4,512]{2,1,0:T(4,128)(2,1)} %reduce_sum.111), calls=%async_computation.6 | async-start | bytes 1048576 | tf_op jit(solution)/shard_map/all_to_all | solution.py:207
  166.3 2.8 fusion.1
  169.1 1.5 copy.39
  170.6 2.4 fusion.15
  173.0 9.9 %scatter_fusion = f32[320,512]{1,0:T(8,128)S(1)} fusion(f32[320,512]{1,0:T(8,128)S(1)} %slice-done, s32[1280]{0:T(1024)S(1)} %copy-done.35, f32[1280,512]{1,0:T(8,128)S(1)} %fusion.15), kind=kCustom, calls=%fused_computation.6 | custom fusion | flops 655360 | bytes 7869440 | tf_op jit(solution)/shard_map/scatter-add | solution.py:202
  182.9 4.6 %all-to-all-done.6 = bf16[128,4,512]{2,1,0:T(4,128)(2,1)} async-done(((bf16[128,4,512]{2,1,0:T(4,128)(2,1)}), bf16[128,4,512]{2,1,0:T(4,128)(2,1)}, u32[]{:S(2)}, u32[]{:S(2)}) %all-to-all-start.6) | async-done | bytes 524320 | tf_op jit(solution)/shard_map/all_to_all | solution.py:207
  187.4 2.1 reshape.187
  189.5 4.8 %scatter_custom_fusion.3 = f32[320,512]{1,0:T(8,128)S(1)} fusion(s32[512]{0:T(512)S(1)} %reshape.185, f32[512,512]{1,0:T(8,128)} %reshape.187, f32[]{:T(128)} %constant.13.clone.1), kind=kCustom, calls=%fused_computation.70 | custom fusion | flops 262144 | bytes 655872 | tf_op jit(solution)/shard_map/scatter-add | solution.py:210
  194.4 4.3 %all_to_all.44 = f32[2,160,512]{2,1,0:T(8,128)S(1)} all-to-all(f32[2,160,512]{2,1,0:T(8,128)S(1)} %bitcast.48), channel_id=1, replica_groups=mesh['nodes'=128,'rep'=2] {'rep'}, dimensions={0} | all-to-all | bytes 1310720 | tf_op jit(solution)/shard_map/all_to_all | solution.py:39
  198.7 1.0 fusion.9
  199.7 209.9 %all-reduce.3.cloned.1.call-done = (f32[1536,512]{1,0:T(8,128)}, f32[512,512]{1,0:T(8,128)}, f32[1024,512]{1,0:T(8,128)}, f32[512,512]{1,0:T(8,128)}) async-done(((f32[1536,512]{1,0:T(8,128)}, f32[512,512]{1,0:T(8,128)}, f32[1024,512]{1,0:T(8,128)}, f32[512,512]{1,0:T(8,128)}), (f32[1536,512]{1,0:T(8,128)}, f32[512,512]{1,0:T(8,128)}, f32[1024,512]{1,0:T(8,128)}, ...) | async-done | bytes 7340048 | tf_op jit(solution)/shard_map/psum | solution.py:219
  409.7 3.6 multiply_convert_fusion
  413.3 0.9 multiply_convert_fusion.5
  414.2 1.3 multiply_convert_fusion.3
  415.5 0.9 multiply_convert_fusion.4
  (123 shorter events, 4.5 us)
Async XLA Ops:
  7.2 62.4 %copy-start = (bf16[512,512]{1,0:T(8,128)(2,1)S(1)}, bf16[512,512]{1,0:T(8,128)(2,1)}, u32[]{:S(2)}) copy-start(bf16[512,512]{1,0:T(8,128)(2,1)} %param.22) | copy-start | bytes 1572868
  8.9 5.0 %all-to-all-start = ((bf16[2,160,512]{2,1,0:T(8,128)(2,1)}), bf16[2,160,512]{2,1,0:T(8,128)(2,1)S(1)}, u32[]{:S(2)}, u32[]{:S(2)}) async-start(bf16[2,160,512]{2,1,0:T(8,128)(2,1)} %broadcast_in_dim.18), calls=%async_computation | async-start | bytes 655360 | tf_op jit(solution)/shard_map/all_to_all | solution.py:16
  13.2 0.8 copy-start.31
  14.0 18.9 %copy-start.35 = (s32[1280]{0:T(1024)S(1)}, s32[1280]{0:T(1024)}, u32[]{:S(2)}) copy-start(s32[1280]{0:T(1024)} %param.19) | copy-start | bytes 15364
  16.8 34.7 %all-to-all-start.1 = ((bf16[128,4,512]{2,1,0:T(4,128)(2,1)}), bf16[128,4,512]{2,1,0:T(4,128)(2,1)}, u32[]{:S(2)}, u32[]{:S(2)}) async-start(bf16[128,4,512]{2,1,0:T(4,128)(2,1)} %reshape.119), calls=%async_computation.1 | async-start | bytes 1048576 | tf_op jit(solution)/shard_map/all_to_all | solution.py:171
  32.7 376.9 %all-reduce.3.cloned.1.call-start = ((), (), s32[]{:S(2)}) async-start(), calls=%async_computation.8 | async-start | bytes 14680064 | tf_op jit(solution)/shard_map/psum | solution.py:219
  32.8 32.5 %collective-permute-start = (bf16[1280,512]{1,0:T(8,128)(2,1)}, bf16[1280,512]{1,0:T(8,128)(2,1)}, u32[]{:S(2)}, u32[]{:S(2)}) collective-permute-start(bf16[1280,512]{1,0:T(8,128)(2,1)} %param.15), channel_id=1, source_target_pairs={{0,1},{1,0},{2,3},{3,2},{4,5},{5,4},{6,7},{7,6},{8,9},{9,8},{10,11... | collective-permute-start | bytes 3932168 | tf_op jit(solution)/shard_map/ppermute | solution.py:11
  37.0 7.9 %copy-start.5 = (bf16[1280,512]{1,0:T(8,128)(2,1)}, bf16[1280,512]{1,0:T(8,128)(2,1)S(1)}, u32[]{:S(2)}) copy-start(bf16[1280,512]{1,0:T(8,128)(2,1)S(1)} %gather_fusion.2) | copy-start | bytes 3932164
  37.1 3.0 copy-start.37
  37.1 3.6 copy-start.11
  37.1 3.5 copy-start.15
  62.9 6.7 %copy-start.7 = (bf16[1280,512]{1,0:T(8,128)(2,1)}, bf16[1280,512]{1,0:T(8,128)(2,1)S(1)}, u32[]{:S(2)}) copy-start(bf16[1280,512]{1,0:T(8,128)(2,1)S(1)} %gather_fusion.1) | copy-start | bytes 3932164
  62.9 2.4 copy-start.10
  69.6 1.2 copy-start.23
  69.6 1.3 copy-start.36
  69.6 1.3 copy-start.38
  87.1 10.8 %copy-start.27 = (bf16[160,512]{1,0:T(8,128)(2,1)S(1)}, bf16[160,512]{1,0:T(8,128)(2,1)}, u32[]{:S(2)}) copy-start(bf16[160,512]{1,0:T(8,128)(2,1)} %param.16) | copy-start | bytes 491524
  87.1 10.9 %copy-start.39 = (f32[512]{0:T(512)S(1)}, f32[512]{0:T(512)}, u32[]{:S(2)}) copy-start(f32[512]{0:T(512)} %param.27) | copy-start | bytes 6148
  94.6 4.0 copy-start.17
  94.6 3.6 copy-start.28
  94.7 3.6 copy-start.44
  96.2 2.5 copy-start.33
  96.2 2.5 copy-start.12
  97.7 5.8 %copy-start.21 = (f32[160,512]{1,0:T(8,128)}, f32[160,512]{1,0:T(8,128)S(1)}, u32[]{:S(2)}) copy-start(f32[160,512]{1,0:T(8,128)S(1)} %get-tuple-element.37) | copy-start | bytes 983044
  98.2 10.0 %copy-start.40 = (f32[160]{0:T(256)}, f32[160]{0:T(256)S(1)}, u32[]{:S(2)}) copy-start(f32[160]{0:T(256)S(1)} %get-tuple-element.38) | copy-start | bytes 1924
  98.2 10.0 %copy-start.42 = (f32[160]{0:T(256)}, f32[160]{0:T(256)S(1)}, u32[]{:S(2)}) copy-start(f32[160]{0:T(256)S(1)} %get-tuple-element.39) | copy-start | bytes 1924
  98.6 0.7 copy-start.19
  110.6 2.7 copy-start.3
  110.6 2.7 copy-start.4
  113.3 1.7 copy-start.45
  115.1 1.5 copy-start.6
  116.6 13.3 %copy-start.9 = (bf16[1280,512]{1,0:T(8,128)(2,1)}, bf16[1280,512]{1,0:T(8,128)(2,1)S(1)}, u32[]{:S(2)}) copy-start(bf16[1280,512]{1,0:T(8,128)(2,1)S(1)} %fusion.2) | copy-start | bytes 3932164
  116.6 1.8 copy-start.8
  118.4 1.3 copy-start.24
  119.7 1.9 copy-start.18
  119.7 1.9 copy-start.20
  119.7 2.3 copy-start.16
  121.6 1.0 copy-start.22
  121.6 1.0 copy-start.29
  121.6 1.1 copy-start.34
  121.6 1.1 copy-start.41
  121.6 1.1 copy-start.43
  144.5 21.8 %copy-start.2 = (f32[1344,512]{1,0:T(8,128)}, f32[1344,512]{1,0:T(8,128)S(1)}, u32[]{:S(2)}) copy-start(f32[1344,512]{1,0:T(8,128)S(1)} %scatter_custom_fusion.1) | copy-start | bytes 8257540
  149.6 16.6 %copy-start.32 = (s32[1,128,4]{2,1,0:T(8,128)S(1)}, s32[1,128,4]{2,1,0:T(8,128)}, u32[]{:S(2)}) copy-start(s32[1,128,4]{2,1,0:T(8,128)} %copy-done.31) | copy-start | bytes 6148
  158.1 29.4 %all-to-all-start.6 = ((bf16[128,4,512]{2,1,0:T(4,128)(2,1)}), bf16[128,4,512]{2,1,0:T(4,128)(2,1)}, u32[]{:S(2)}, u32[]{:S(2)}) async-start(bf16[128,4,512]{2,1,0:T(4,128)(2,1)} %reduce_sum.111), calls=%async_computation.6 | async-start | bytes 1048576 | tf_op jit(solution)/shard_map/all_to_all | solution.py:207
  170.6 2.4 slice-start
  189.5 9.2 %copy-start.13 = (bf16[1024,512]{1,0:T(8,128)(2,1)S(1)}, bf16[1024,512]{1,0:T(8,128)(2,1)}, u32[]{:S(2)}) copy-start(bf16[1024,512]{1,0:T(8,128)(2,1)} %param.25) | copy-start | bytes 3145732
  189.5 9.2 %copy-start.30 = (bf16[160,512]{1,0:T(8,128)(2,1)S(1)}, bf16[160,512]{1,0:T(8,128)(2,1)}, u32[]{:S(2)}) copy-start(bf16[160,512]{1,0:T(8,128)(2,1)} %param.16) | copy-start | bytes 491524
  409.7 3.6 copy-start.26
  409.7 4.6 %copy-start.14 = (f32[1024,512]{1,0:T(8,128)S(1)}, f32[1024,512]{1,0:T(8,128)}, u32[]{:S(2)}) copy-start(f32[1024,512]{1,0:T(8,128)} %get-tuple-element.30) | copy-start | bytes 6291460
  413.3 2.2 copy-start.25
  413.3 3.1 copy-start.1
Sparse Core Ops, SparseCore 0:
  130.0 279.6 all-reduce.2
where the time goes:
time: 430 us; the launch traced here: 424 us
  waiting for transfers between devices  222 us (52%)
  other arithmetic  58.3 us (14%)
  local copies, waits for them, and re-layouts  40.9 us (10%)
  matrix products  34.6 us (8%)
  starting transfers between devices  27.6 us (6%)
  blocking collectives  25.5 us (6%)
  between operations  15 us (3%)
    psum x1, waiting for transfers between devices, shards(): lax.psum((weight_grads[0], weight_grads[1], weight_grads[2], weight_grads...  210 us
    all_to_all x1, starting transfers between devices, shards(): lax.all_to_all(outgoing, 'nodes', split_axis=0, concat_axis=0, tiled=True)  15.9 us
    dot_general x7, matrix products, mat_mul(): return jnp.dot(left, right, preferred_element_type=jnp.float32)  14.9 us
    dot_general x7, matrix products, mat_nt(): lax.dot_general(left, right, (((1,), (1,)), ((), ())), preferred_element_...  11.8 us
    scatter-add x1, other arithmetic, shards(): jax.ops.segment_sum(send_grad, senders, num_segments=node_table.shape[0])  11.1 us
    scatter-add x1, other arithmetic, shards(): jax.ops.segment_sum(message, receivers, num_segments=part_rows)  11.1 us
    all_to_all x2, blocking collectives, summed_on_arrival(): lax.all_to_all(split_up(array, dim, devices), axis, 0, 0, tiled=True)  10.6 us
    scatter-add x1, other arithmetic, shards(): jax.ops.segment_sum(recv_grad, receivers, num_segments=part_rows)  9.89 us
  transfers between devices with their start and end apart: 5, of which 4 were waited for; matrix products, arithmetic and copies ran while one was open for 16% of the time, Pallas kernels for 0%

commit v1 on v0

--- a/solution.py
+++ b/solution.py
@@ -217,7 +217,8 @@
     edge_scale = 1.0 / math.sqrt(senders.shape[0] * device_count)
     node_scale = 1.0 / math.sqrt(node_latent.shape[0] * device_count)
     weight_total = lax.psum(
-        (weight_grads[0], weight_grads[1], weight_grads[2], weight_grads[3]), ("nodes", "rep")
+        lax.psum((weight_grads[0], weight_grads[1], weight_grads[2], weight_grads[3]), "nodes"),
+        "rep",
     )
     return (
         grad_nodes,

time: 430 us -> 470 us (1.093)
  waiting for transfers between devices: 222 us -> 256 us
    psum x1, waiting for transfers between devices: 210 us -> 248 us  [shards(): lax.psum((weight_grads[0], weight_grads[1], weight_grads[2], weight_grads...]
  transfers between devices with their start and end apart: 5 -> 6, of which waited for: 4 -> 4; matrix products, arithmetic and copies ran while one was open for 16% -> 15% of each run, Pallas kernels for 0% -> 0%
where the time goes in v1:
time: 470 us; the launch traced here: 462 us
  waiting for transfers between devices  256 us (54%)
  other arithmetic  58.1 us (12%)
  local copies, waits for them, and re-layouts  41.6 us (9%)
  matrix products  35 us (7%)
  starting transfers between devices  31 us (7%)
  blocking collectives  25.5 us (5%)
  between operations  15 us (3%)
    psum x1, waiting for transfers between devices, shards(): lax.psum((weight_grads[0], weight_grads[1], weight_grads[2], weight_grads...  248 us
    all_to_all x1, starting transfers between devices, shards(): lax.all_to_all(outgoing, 'nodes', split_axis=0, concat_axis=0, tiled=True)  15.9 us
    dot_general x7, matrix products, mat_mul(): return jnp.dot(left, right, preferred_element_type=jnp.float32)  14.9 us
    dot_general x7, matrix products, mat_nt(): lax.dot_general(left, right, (((1,), (1,)), ((), ())), preferred_element_...  12.2 us
    all_to_all x1, starting transfers between devices, shards(): lax.all_to_all(paired.astype(jnp.bfloat16), 'nodes', split_axis=0, concat...  11.3 us
    scatter-add x1, other arithmetic, shards(): jax.ops.segment_sum(message, receivers, num_segments=part_rows)  11.1 us
    scatter-add x1, other arithmetic, shards(): jax.ops.segment_sum(send_grad, senders, num_segments=node_table.shape[0])  10.9 us
    all_to_all x2, blocking collectives, summed_on_arrival(): lax.all_to_all(split_up(array, dim, devices), axis, 0, 0, tiled=True)  10.6 us
  transfers between devices with their start and end apart: 6, of which 4 were waited for; matrix products, arithmetic and copies ran while one was open for 15% of the time, Pallas kernels for 0%

profile of v1, /device:TPU:2, one launch (start us, length us, event | category | flops | bytes accessed | tf_op | source)
XLA Modules:
  0.0 462.4 jit_solution(16204627394645984807)
XLA Ops:
  7.2 1.7 broadcast_in_dim.18
  8.9 3.5 all-to-all-start
  12.4 0.7 constant_dynamic-slice_fusion
  13.3 0.6 all-to-all-done
  14.0 2.0 gather_fusion
  15.9 0.9 reshape.119
  16.8 15.9 %all-to-all-start.1 = ((bf16[128,4,512]{2,1,0:T(4,128)(2,1)}), bf16[128,4,512]{2,1,0:T(4,128)(2,1)}, u32[]{:S(2)}, u32[]{:S(2)}) async-start(bf16[128,4,512]{2,1,0:T(4,128)(2,1)} %reshape.119), calls=%async_computation.1 | async-start | bytes 1048576 | tf_op jit(solution)/shard_map/all_to_all | solution.py:171
  32.9 4.1 gather_fusion.2
  37.1 2.9 copy.33
  40.0 0.6 pad_clamp_fusion.1
  40.6 1.0 fusion.13
  41.6 3.4 fusion.17
  45.0 6.5 %all-to-all-done.1 = bf16[128,4,512]{2,1,0:T(4,128)(2,1)} async-done(((bf16[128,4,512]{2,1,0:T(4,128)(2,1)}), bf16[128,4,512]{2,1,0:T(4,128)(2,1)}, u32[]{:S(2)}, u32[]{:S(2)}) %all-to-all-start.1) | async-done | bytes 524320 | tf_op jit(solution)/shard_map/all_to_all | solution.py:171
  51.5 1.3 broadcast_in_dim.19
  52.8 4.9 %all_to_all.40 = bf16[2,128,4,512]{3,2,1,0:T(4,128)(2,1)S(1)} all-to-all(bf16[2,128,4,512]{3,2,1,0:T(4,128)(2,1)S(1)} %broadcast_in_dim.19), channel_id=1, replica_groups=mesh['nodes'=128,'rep'=2] {'rep'}, dimensions={0} | all-to-all | bytes 2097152 | tf_op jit(solution)/shard_map/all_to_all | solution.py:16
  58.4 4.2 gather_fusion.1
  62.7 2.4 fusion.21
  65.1 4.2 multiply_convert_fusion.2
  69.4 0.9 fusion.43
  70.6 1.9 multiply_add_fusion
  72.6 3.2 copy.34
  75.8 11.1 %scatter_custom_fusion = f32[320,512]{1,0:T(8,128)} fusion(s32[1280]{0:T(1024)S(1)} %copy-done.35, f32[1280,512]{1,0:T(8,128)} %copy.34, f32[]{:T(128)} %constant.13.clone.1), kind=kCustom, calls=%fused_computation.72 | custom fusion | flops 655360 | bytes 655872 | tf_op jit(solution)/shard_map/scatter-add | solution.py:181
  86.9 6.3 %all_to_all.41 = f32[2,160,512]{2,1,0:T(8,128)} all-to-all(f32[2,160,512]{2,1,0:T(8,128)} %bitcast.47), channel_id=1, replica_groups=mesh['nodes'=128,'rep'=2] {'rep'}, dimensions={0} | all-to-all | bytes 1310720 | tf_op jit(solution)/shard_map/all_to_all | solution.py:39
  93.2 1.2 reduce_sum.104
  94.4 1.5 convolution_add_fusion.3
  95.9 1.5 fusion.44
  99.1 4.5 all_to_all.42
  103.6 4.7 %gather_fusion.3 = bf16[1280,512]{1,0:T(8,128)(2,1)} fusion(bf16[320,512]{1,0:T(8,128)(2,1)S(1)} %bitcast.44, s32[2048]{0:T(1024)S(1)} %pad_clamp_fusion), kind=kCustom, calls=%fused_computation.3 | custom fusion | bytes 2626560 | tf_op jit(solution)/shard_map/gather | solution.py:187
  108.3 2.4 copy.35
  110.7 2.7 fusion.4
  113.4 1.0 multiply_convert_fusion.1
  114.4 0.7 copy-done.45
  115.2 1.5 fusion.2
  116.7 0.9 fusion.46
  117.6 0.9 copy-done.8
  118.5 0.9 fusion.45
  119.4 0.4 copy-done.24
  119.8 1.9 fusion.47
  122.8 1.4 fusion.39
  124.3 1.5 pad_maximum_fusion.1
  125.8 2.2 convolution_bitcast_fusion
  128.0 2.0 pad_maximum_fusion
  130.2 247.6 %all-reduce.5.cloned.1.call-done = (f32[1536,512]{1,0:T(8,128)}, f32[512,512]{1,0:T(8,128)}, f32[1024,512]{1,0:T(8,128)}, f32[512,512]{1,0:T(8,128)}) async-done(((f32[1536,512]{1,0:T(8,128)}, f32[512,512]{1,0:T(8,128)}, f32[1024,512]{1,0:T(8,128)}, f32[512,512]{1,0:T(8,128)}), (f32[1536,512]{1,0:T(8,128)}, f32[512,512]{1,0:T(8,128)}, f32[1024,512]{1,0:T(8,128)}, ...) | async-done | bytes 7340048 | tf_op jit(solution)/shard_map/psum | solution.py:220
  377.9 3.5 fusion.19
  381.4 10.9 %scatter_custom_fusion.1 = f32[1344,512]{1,0:T(8,128)S(1)} fusion(s32[1280]{0:T(1024)} %param.18, f32[1280,512]{1,0:T(8,128)} %fusion.19, f32[]{:T(128)} %constant.13.clone.1), kind=kCustom, calls=%fused_computation.30 | custom fusion | flops 655360 | bytes 2753024 | tf_op jit(solution)/shard_map/scatter-add | solution.py:201
  392.3 1.2 slice.65
  393.5 2.8 convert_element_type.72
  396.3 1.8 copy.42
  398.1 5.5 %all_to_all.43 = bf16[2,128,4,512]{3,2,1,0:T(4,128)(2,1)} all-to-all(bf16[2,128,4,512]{3,2,1,0:T(4,128)(2,1)S(1)} %bitcast.46), channel_id=1, replica_groups=mesh['nodes'=128,'rep'=2] {'rep'}, dimensions={0} | all-to-all | bytes 2097152 | tf_op jit(solution)/shard_map/all_to_all | solution.py:45
  403.7 2.9 reduce_sum.111
  406.5 11.3 %all-to-all-start.6 = ((bf16[128,4,512]{2,1,0:T(4,128)(2,1)}), bf16[128,4,512]{2,1,0:T(4,128)(2,1)}, u32[]{:S(2)}, u32[]{:S(2)}) async-start(bf16[128,4,512]{2,1,0:T(4,128)(2,1)} %reduce_sum.111), calls=%async_computation.6 | async-start | bytes 1048576 | tf_op jit(solution)/shard_map/all_to_all | solution.py:207
  418.0 3.1 fusion.1
  421.1 1.5 copy.39
  422.6 2.5 fusion.15
  425.1 10.1 %scatter_fusion = f32[320,512]{1,0:T(8,128)S(1)} fusion(f32[320,512]{1,0:T(8,128)S(1)} %slice-done, s32[1280]{0:T(1024)S(1)} %copy-done.35, f32[1280,512]{1,0:T(8,128)S(1)} %fusion.15), kind=kCustom, calls=%fused_computation.6 | custom fusion | flops 655360 | bytes 7869440 | tf_op jit(solution)/shard_map/scatter-add | solution.py:202
  435.2 1.4 all-to-all-done.6
  436.6 2.1 reshape.187
  438.6 4.5 scatter_custom_fusion.3
  443.3 4.3 all_to_all.44
  447.6 1.0 fusion.9
  448.6 3.6 multiply_convert_fusion
  452.2 0.9 multiply_convert_fusion.5
  453.2 1.3 multiply_convert_fusion.3
  454.4 0.9 multiply_convert_fusion.4
  (126 shorter events, 4.7 us)
Async XLA Ops:
  7.2 62.2 %copy-start = (bf16[512,512]{1,0:T(8,128)(2,1)S(1)}, bf16[512,512]{1,0:T(8,128)(2,1)}, u32[]{:S(2)}) copy-start(bf16[512,512]{1,0:T(8,128)(2,1)} %param.22) | copy-start | bytes 1572868
  8.9 5.0 %all-to-all-start = ((bf16[2,160,512]{2,1,0:T(8,128)(2,1)}), bf16[2,160,512]{2,1,0:T(8,128)(2,1)S(1)}, u32[]{:S(2)}, u32[]{:S(2)}) async-start(bf16[2,160,512]{2,1,0:T(8,128)(2,1)} %broadcast_in_dim.18), calls=%async_computation | async-start | bytes 655360 | tf_op jit(solution)/shard_map/all_to_all | solution.py:16
  13.2 0.8 copy-start.31
  14.0 18.9 %copy-start.35 = (s32[1280]{0:T(1024)S(1)}, s32[1280]{0:T(1024)}, u32[]{:S(2)}) copy-start(s32[1280]{0:T(1024)} %param.19) | copy-start | bytes 15364
  16.8 34.7 %all-to-all-start.1 = ((bf16[128,4,512]{2,1,0:T(4,128)(2,1)}), bf16[128,4,512]{2,1,0:T(4,128)(2,1)}, u32[]{:S(2)}, u32[]{:S(2)}) async-start(bf16[128,4,512]{2,1,0:T(4,128)(2,1)} %reshape.119), calls=%async_computation.1 | async-start | bytes 1048576 | tf_op jit(solution)/shard_map/all_to_all | solution.py:171
  32.7 345.1 %all-reduce.5.cloned.1.call-start = ((), (), s32[]{:S(2)}) async-start(), calls=%async_computation.8 | async-start | bytes 14680064 | tf_op jit(solution)/shard_map/psum | solution.py:220
  32.8 32.3 %collective-permute-start = (bf16[1280,512]{1,0:T(8,128)(2,1)}, bf16[1280,512]{1,0:T(8,128)(2,1)}, u32[]{:S(2)}, u32[]{:S(2)}) collective-permute-start(bf16[1280,512]{1,0:T(8,128)(2,1)} %param.15), channel_id=1, source_target_pairs={{0,1},{1,0},{2,3},{3,2},{4,5},{5,4},{6,7},{7,6},{8,9},{9,8},{10,11... | collective-permute-start | bytes 3932168 | tf_op jit(solution)/shard_map/ppermute | solution.py:11
  37.0 7.9 %copy-start.5 = (bf16[1280,512]{1,0:T(8,128)(2,1)}, bf16[1280,512]{1,0:T(8,128)(2,1)S(1)}, u32[]{:S(2)}) copy-start(bf16[1280,512]{1,0:T(8,128)(2,1)S(1)} %gather_fusion.2) | copy-start | bytes 3932164
  37.1 2.9 copy-start.37
  37.1 3.5 copy-start.11
  37.1 3.5 copy-start.15
  62.7 6.7 %copy-start.7 = (bf16[1280,512]{1,0:T(8,128)(2,1)}, bf16[1280,512]{1,0:T(8,128)(2,1)S(1)}, u32[]{:S(2)}) copy-start(bf16[1280,512]{1,0:T(8,128)(2,1)S(1)} %gather_fusion.1) | copy-start | bytes 3932164
  62.7 2.4 copy-start.10
  69.4 1.2 copy-start.23
  69.4 1.3 copy-start.36
  69.4 1.3 copy-start.38
  86.9 10.8 %copy-start.27 = (bf16[160,512]{1,0:T(8,128)(2,1)S(1)}, bf16[160,512]{1,0:T(8,128)(2,1)}, u32[]{:S(2)}) copy-start(bf16[160,512]{1,0:T(8,128)(2,1)} %param.16) | copy-start | bytes 491524
  86.9 10.8 %copy-start.39 = (f32[512]{0:T(512)S(1)}, f32[512]{0:T(512)}, u32[]{:S(2)}) copy-start(f32[512]{0:T(512)} %param.27) | copy-start | bytes 6148
  94.4 4.0 copy-start.17
  94.4 3.6 copy-start.28
  94.4 3.6 copy-start.44
  95.9 2.5 copy-start.33
  95.9 2.5 copy-start.12
  97.5 6.1 %copy-start.21 = (f32[160,512]{1,0:T(8,128)}, f32[160,512]{1,0:T(8,128)S(1)}, u32[]{:S(2)}) copy-start(f32[160,512]{1,0:T(8,128)S(1)} %get-tuple-element.41) | copy-start | bytes 983044
  97.9 10.3 %copy-start.40 = (f32[160]{0:T(256)}, f32[160]{0:T(256)S(1)}, u32[]{:S(2)}) copy-start(f32[160]{0:T(256)S(1)} %get-tuple-element.42) | copy-start | bytes 1924
  98.0 10.3 %copy-start.42 = (f32[160]{0:T(256)}, f32[160]{0:T(256)S(1)}, u32[]{:S(2)}) copy-start(f32[160]{0:T(256)S(1)} %get-tuple-element.43) | copy-start | bytes 1924
  98.4 0.7 copy-start.19
  110.7 2.7 copy-start.3
  110.7 2.7 copy-start.4
  113.4 1.7 copy-start.45
  115.2 1.5 copy-start.6
  116.7 261.2 %copy-start.9 = (bf16[1280,512]{1,0:T(8,128)(2,1)}, bf16[1280,512]{1,0:T(8,128)(2,1)S(1)}, u32[]{:S(2)}) copy-start(bf16[1280,512]{1,0:T(8,128)(2,1)S(1)} %fusion.2) | copy-start | bytes 3932164
  116.7 1.8 copy-start.8
  118.5 1.3 copy-start.24
  119.8 1.9 copy-start.18
  119.8 1.9 copy-start.20
  119.8 2.3 copy-start.16
  121.7 1.0 copy-start.22
  121.7 1.0 copy-start.29
  121.7 1.1 copy-start.34
  121.7 1.1 copy-start.41
  121.7 1.1 copy-start.43
  130.0 318.6 %all-reduce.7.cloned.1.call-start = ((), (), s32[]{:S(2)}) async-start(), calls=%async_computation.9 | async-start | bytes 14680064 | tf_op jit(solution)/shard_map/psum | solution.py:219
  392.3 25.7 %copy-start.2 = (f32[1344,512]{1,0:T(8,128)}, f32[1344,512]{1,0:T(8,128)S(1)}, u32[]{:S(2)}) copy-start(f32[1344,512]{1,0:T(8,128)S(1)} %scatter_custom_fusion.1) | copy-start | bytes 8257540
  398.1 19.7 %copy-start.32 = (s32[1,128,4]{2,1,0:T(8,128)S(1)}, s32[1,128,4]{2,1,0:T(8,128)}, u32[]{:S(2)}) copy-start(s32[1,128,4]{2,1,0:T(8,128)} %copy-done.31) | copy-start | bytes 6148
  406.5 30.0 %all-to-all-start.6 = ((bf16[128,4,512]{2,1,0:T(4,128)(2,1)}), bf16[128,4,512]{2,1,0:T(4,128)(2,1)}, u32[]{:S(2)}, u32[]{:S(2)}) async-start(bf16[128,4,512]{2,1,0:T(4,128)(2,1)} %reduce_sum.111), calls=%async_computation.6 | async-start | bytes 1048576 | tf_op jit(solution)/shard_map/all_to_all | solution.py:207
  422.6 2.5 slice-start
  438.6 8.9 %copy-start.13 = (bf16[1024,512]{1,0:T(8,128)(2,1)S(1)}, bf16[1024,512]{1,0:T(8,128)(2,1)}, u32[]{:S(2)}) copy-start(bf16[1024,512]{1,0:T(8,128)(2,1)} %param.25) | copy-start | bytes 3145732
  438.6 8.9 %copy-start.30 = (bf16[160,512]{1,0:T(8,128)(2,1)S(1)}, bf16[160,512]{1,0:T(8,128)(2,1)}, u32[]{:S(2)}) copy-start(bf16[160,512]{1,0:T(8,128)(2,1)} %param.16) | copy-start | bytes 491524
  448.6 3.6 copy-start.26
  448.6 4.6 copy-start.14
  452.2 2.2 copy-start.25
  452.2 3.1 copy-start.1
Sparse Core Ops, SparseCore 0:
  130.1 247.6 all-reduce.4
  381.2 43.4 all-reduce.6
